TPU v7x, 768 devices: a whole 4x8x12 slice. The times are simulated.
768 devices in a mesh: blk: 32 (over x, y_lo, core), grp: 24 (over y_hi, z).
Axes of the slice: x: 4, y: 8 (y_hi: 2, y_lo: 4; y = y_hi * 4 + y_lo), z: 12, core: 2. Of those that a mesh axis runs over, the one named last changes fastest.
Arguments:
- query_rows: bfloat16 [393216, 1024], P(('blk', 'grp')), may hold values from -8 to 8
- key_rows: bfloat16 [393216, 1024], P(('blk', 'grp')), may hold values from -8 to 8
- value_rows: bfloat16 [393216, 1024], P(('blk', 'grp')), may hold values from -6 to 6
- tile_lists: int32 [3072, 9], P(('blk', 'grp')), may hold values from -1 to 3071, as said below
- hilbert_order: int32 [393216], P(('blk', 'grp')), may hold values from 0 to 393215, as said below
Outputs:
- attention_out: bfloat16 [393216, 1024], P(('blk', 'grp'))
Inputs may be any that keep to these rules, and one draw needn't show every extreme that they name: `tile_lists`: row r lists the key tiles of query tile r. Slot j for j <= 4 holds r - 2 + j or -1; slot 5 + g holds global tile g, the same in every row, the global tiles lying 768 apart. No tile appears twice in a row, and tile r appears in row r. `hilbert_order`: A permutation that maps each aligned block of 512 positions onto itself.
All inputs are finite; a program needn't handle non-finite values.
Results may differ from a plain program's by a relative error of at most 0.0049.
Values may be sent and summed in bfloat16 or wider, within the bound.
A program may use at most 64 MiB of HBM per device.

v0:
```python
import jax
import jax.numpy as jnp
from jax import lax
from jax.sharding import PartitionSpec as P

LOCAL_HEADS = 8
HEAD_WIDTH = 128
TILE_POINTS = 128
BAND = 2
NG = 4


def extended(block, sides, width):
    for axis, dim in sides:
        count = lax.axis_size(axis)
        forward = [(i, i + 1) for i in range(count - 1)]
        backward = [(target, source) for source, target in forward]
        low = lax.ppermute(
            lax.slice_in_dim(block, block.shape[dim] - width, None, axis=dim), axis, forward
        )
        high = lax.ppermute(lax.slice_in_dim(block, 0, width, axis=dim), axis, backward)
        block = jnp.concatenate([low, block, high], axis=dim)
    return block


def spread(array, axis, root):
    mine = lax.axis_index(axis) == root
    return lax.psum(jnp.where(mine, array, jnp.zeros_like(array)), axis)


def body(query_rows, key_rows, value_rows, tile_lists, hilbert_order):
    row_count = query_rows.shape[0]
    feature_count = query_rows.shape[1]
    tiles_here = row_count // TILE_POINTS
    local_order = hilbert_order % row_count
    q_sorted = query_rows[local_order]
    kv_sorted = jnp.stack([key_rows[local_order], value_rows[local_order]])
    padded = extended(kv_sorted, ((("blk", "grp"), 1),), BAND * TILE_POINTS)
    global_ids = tile_lists[0, 2 * BAND + 1 :]
    fetched = []
    for member in range(NG):
        tile_id = global_ids[member]
        owner_index = tile_id // tiles_here
        start_row = tile_id % tiles_here * TILE_POINTS
        tile_block = lax.dynamic_slice_in_dim(kv_sorted, start_row, TILE_POINTS, 1)
        fetched.append(spread(tile_block, ("blk", "grp"), owner_index))
    global_kv = jnp.concatenate(fetched, axis=1)
    band_valid = tile_lists[:, : 2 * BAND + 1] >= 0
    query_tiles = q_sorted.reshape(tiles_here, TILE_POINTS, LOCAL_HEADS, HEAD_WIDTH)
    global_ok = jnp.ones((NG * TILE_POINTS,), dtype=bool)
    score_scale = HEAD_WIDTH ** (-0.5)

    def one_tile(inputs):
        tile_number, queries_here, valid_here = inputs
        band_kv = lax.dynamic_slice_in_dim(
            padded, tile_number * TILE_POINTS, (2 * BAND + 1) * TILE_POINTS, 1
        )
        kv_here = jnp.concatenate([band_kv, global_kv], axis=1)
        key_heads = kv_here[0].reshape(-1, LOCAL_HEADS, HEAD_WIDTH)
        value_heads = kv_here[1].reshape(-1, LOCAL_HEADS, HEAD_WIDTH)
        allowed = jnp.concatenate([jnp.repeat(valid_here, TILE_POINTS), global_ok])
        scores = (
            jnp.einsum("qhd,khd->hqk", queries_here, key_heads, preferred_element_type=jnp.float32)
            * score_scale
        )
        scores = jnp.where(allowed[None, None, :], scores, -1e30)
        row_peak = jnp.max(scores, axis=-1, keepdims=True)
        exponent = jnp.exp(scores - row_peak)
        weights = (exponent / jnp.sum(exponent, axis=-1, keepdims=True)).astype(jnp.bfloat16)
        attended = jnp.einsum(
            "hqk,khd->qhd", weights, value_heads, preferred_element_type=jnp.float32
        )
        return attended.reshape(TILE_POINTS, feature_count).astype(jnp.bfloat16)

    tile_numbers = jnp.arange(tiles_here, dtype=jnp.int32)
    attended = lax.map(one_tile, (tile_numbers, query_tiles, band_valid)).reshape(
        row_count, feature_count
    )
    return jnp.zeros_like(attended).at[local_order].set(attended)


def solution(mesh):
    in_specs = (
        P(("blk", "grp"), None),
        P(("blk", "grp"), None),
        P(("blk", "grp"), None),
        P(("blk", "grp"), None),
        P(("blk", "grp")),
    )
    out_specs = P(("blk", "grp"), None)
    return jax.shard_map(body, mesh=mesh, in_specs=in_specs, out_specs=out_specs, check_vma=False)
```

profile of v0, /device:TPU:1, one launch (start us, length us, event | category | flops | bytes accessed | tf_op | source)
XLA Modules:
  0.0 729.1 jit_solution(17816670538708779771)
XLA Ops:
  6.5 1.5 fusion.22
  18.9 2.1 gather_fusion
  21.0 2.8 gather_fusion.1
  23.8 3.0 fusion.11
  26.8 2.7 fusion.8
  29.5 4.8 collective-permute-start
  34.4 18.2 %collective-permute-start.1 = (bf16[2,256,1024]{2,1,0:T(8,128)(2,1)}, bf16[2,256,1024]{2,1,0:T(8,128)(2,1)}, u32[]{:S(2)}, u32[]{:S(2)}) collective-permute-start(bf16[2,256,1024]{2,1,0:T(8,128)(2,1)} %get-tuple-element.119), channel_id=1, source_target_pairs={{1,0},{2,1},{3,2},{4,3},{5,4},{6,5},{7,6},{8,7},{9,8},{10,9},{11,1... | collective-permute-start | bytes 3145736 | tf_op jit(solution)/shard_map/ppermute | solution.py:21
  52.6 2.8 gather_fusion.2
  55.4 2.6 copy.33
  58.0 518.8 %all-reduce.4.cloned.1.call-done = (bf16[2,128,1024]{2,1,0:T(8,128)(2,1)}, bf16[2,128,1024]{2,1,0:T(8,128)(2,1)}, bf16[2,128,1024]{2,1,0:T(8,128)(2,1)}, bf16[2,128,1024]{2,1,0:T(8,128)(2,1)}) async-done(((bf16[2,128,1024]{2,1,0:T(8,128)(2,1)}, bf16[2,128,1024]{2,1,0:T(8,128)(2,1)}, bf16[2,128,1024]{2,1,0:T(8,128)(2,1)}, bf16[2,128,1024]{2,1,0:T(8,128)(2,1)}), (bf16[2,128,1024]{2,1,0:T(8,128)(2,1)}, ...) | async-done | bytes 2097168 | tf_op jit(solution)/shard_map/psum | solution.py:28
  576.9 2.0 copy.22
  578.9 2.0 copy.23
  581.0 2.0 copy.24
  583.0 2.0 copy.25
  585.1 3.5 pad_maximum_fusion
  588.6 129.5 %while.10 = (s32[]{:T(128)}, bf16[4,128,1024]{2,1,0:T(8,128)(2,1)}, s32[4]{0:T(128)S(1)}, bf16[2,1024,1024]{2,1,0:T(8,128)(2,1)}, bf16[2,128,1024]{1,2,0:T(8,128...) while((s32[]{:T(128)}, bf16[4,128,1024]{2,1,0:T(8,128)(2,1)}, ...), condition=%wide.region_7.8_spmd, body=%wide.region_4.7_spmd.sunk | while | flops 916720896 | bytes 49296764 | solution.py:76
  589.8 3.5 constant_dynamic-slice_fusion.4
  593.4 4.4 copy.46
  597.8 2.0 constant_dynamic-update-slice_fusion.12
  599.8 1.2 constant_dynamic-update-slice_fusion.13
  600.9 1.2 constant_dynamic-update-slice_fusion.14
  602.1 1.2 constant_dynamic-update-slice_fusion.15
  603.3 1.2 constant_dynamic-update-slice_fusion.16
  604.4 1.7 fusion.38
  606.2 1.0 constant_dynamic-slice_fusion.5
  607.9 3.0 fusion.39
  610.9 2.6 exponential_reduce_fusion.2
  613.5 6.6 fusion.40
  622.2 3.5 constant_dynamic-slice_fusion.4
  625.7 4.4 copy.46
  630.2 2.0 constant_dynamic-update-slice_fusion.12
  632.1 1.2 constant_dynamic-update-slice_fusion.13
  633.3 1.2 constant_dynamic-update-slice_fusion.14
  634.5 1.2 constant_dynamic-update-slice_fusion.15
  635.6 1.2 constant_dynamic-update-slice_fusion.16
  636.8 1.7 fusion.38
  638.6 1.0 constant_dynamic-slice_fusion.5
  640.2 3.0 fusion.39
  643.2 2.6 exponential_reduce_fusion.2
  645.8 6.6 fusion.40
  654.5 3.5 constant_dynamic-slice_fusion.4
  658.1 4.4 copy.46
  662.5 2.0 constant_dynamic-update-slice_fusion.12
  664.5 1.2 constant_dynamic-update-slice_fusion.13
  665.7 1.2 constant_dynamic-update-slice_fusion.14
  666.8 1.2 constant_dynamic-update-slice_fusion.15
  668.0 1.2 constant_dynamic-update-slice_fusion.16
  669.2 1.7 fusion.38
  670.9 1.0 constant_dynamic-slice_fusion.5
  672.6 3.0 fusion.39
  675.6 2.6 exponential_reduce_fusion.2
  678.2 6.6 fusion.40
  686.9 3.5 constant_dynamic-slice_fusion.4
  690.4 4.4 copy.46
  694.9 2.0 constant_dynamic-update-slice_fusion.12
  696.8 1.2 constant_dynamic-update-slice_fusion.13
  698.0 1.2 constant_dynamic-update-slice_fusion.14
  699.2 1.2 constant_dynamic-update-slice_fusion.15
  700.4 1.2 constant_dynamic-update-slice_fusion.16
  701.5 1.7 fusion.38
  704.9 3.0 fusion.39
  708.0 2.6 exponential_reduce_fusion.2
  710.5 6.6 fusion.40
  718.0 4.2 scatter_custom_fusion
  (52 shorter events, 10.3 us)
Async XLA Ops:
  6.5 12.4 %copy-start = (bf16[512,1024]{1,0:T(8,128)(2,1)S(1)}, bf16[512,1024]{1,0:T(8,128)(2,1)}, u32[]{:S(2)}) copy-start(bf16[512,1024]{1,0:T(8,128)(2,1)} %param.8) | copy-start | bytes 3145732
  6.5 570.3 %all-reduce.4.cloned.1.call-start = ((), (), s32[]{:S(2)}) async-start(), calls=%async_computation | async-start | bytes 4194304 | tf_op jit(solution)/shard_map/psum | solution.py:28
  18.9 2.1 copy-start.1
  23.8 28.8 %copy-start.2 = (bf16[512,1024]{1,0:T(8,128)(2,1)S(1)}, bf16[512,1024]{1,0:T(8,128)(2,1)}, u32[]{:S(2)}) copy-start(bf16[512,1024]{1,0:T(8,128)(2,1)} %param.7) | copy-start | bytes 3145732
  29.5 555.5 %collective-permute-start = (bf16[2,256,1024]{2,1,0:T(8,128)(2,1)}, bf16[2,256,1024]{2,1,0:T(8,128)(2,1)}, u32[]{:S(2)}, u32[]{:S(2)}) collective-permute-start(bf16[2,256,1024]{2,1,0:T(8,128)(2,1)} %get-tuple-element.118), channel_id=1, source_target_pairs={{0,1},{1,2},{2,3},{3,4},{4,5},{5,6},{6,7},{7,8},{8,9},{9,10},{10,1... | collective-permute-start | bytes 3145736 | tf_op jit(solution)/shard_map/ppermute | solution.py:18
  34.4 550.7 %collective-permute-start.1 = (bf16[2,256,1024]{2,1,0:T(8,128)(2,1)}, bf16[2,256,1024]{2,1,0:T(8,128)(2,1)}, u32[]{:S(2)}, u32[]{:S(2)}) collective-permute-start(bf16[2,256,1024]{2,1,0:T(8,128)(2,1)} %get-tuple-element.119), channel_id=1, source_target_pairs={{1,0},{2,1},{3,2},{4,3},{5,4},{6,5},{7,6},{8,7},{9,8},{10,9},{11,1... | collective-permute-start | bytes 3145736 | tf_op jit(solution)/shard_map/ppermute | solution.py:21
  52.6 5.4 copy-start.5
  55.4 529.6 %copy-start.4 = (bf16[512,1024]{1,0:T(8,128)(2,1)S(1)}, bf16[512,1024]{1,0:T(8,128)(2,1)}, u32[]{:S(2)}) copy-start(bf16[512,1024]{1,0:T(8,128)(2,1)} %gather_fusion.1) | copy-start | bytes 3145732
  607.2 0.7 copy-start.3
  639.5 0.7 copy-start.3
  671.9 0.7 copy-start.3
  704.2 0.7 copy-start.3
Sparse Core Ops, SparseCore 0:
  26.9 549.8 all-reduce.3
where the time goes:
time: 733 us; the launch traced here: 729 us
  waiting for transfers between devices  519 us (71%)
  local copies, waits for them, and re-layouts  102 us (14%)
  matrix products  48.7 us (7%)
  between operations  23.7 us (3%)
  starting transfers between devices  23.1 us (3%)
  other arithmetic  9.93 us (1%)
    psum x1, waiting for transfers between devices, spread(): return lax.psum(jnp.where(mine, array, jnp.zeros_like(array)), axis)  519 us
    dynamic_slice x8, local copies, waits for them, and re-layouts, one_tile(): lax.dynamic_slice_in_dim(padded, tile_number * TILE_POINTS, (2 * BAND + 1...  31.9 us
    dot_general x4, matrix products, one_tile(): jnp.einsum('hqk,khd->qhd', weights, value_heads, preferred_element_type=j...  26.4 us
    while x24, local copies, waits for them, and re-layouts  24.3 us
    ppermute x1, starting transfers between devices, extended(): lax.ppermute(lax.slice_in_dim(block, 0, width, axis=dim), axis, backward)  18.2 us
  transfers between devices with their start and end apart: 3, of which 1 were waited for; matrix products, arithmetic and copies ran while one was open for 2% of the time, Pallas kernels for 0%

commit v1 on v0

v1 whole, which is shorter than its diff:
```python
import functools

import jax
import jax.numpy as jnp
from jax import lax
from jax.experimental import pallas as pl
from jax.experimental.pallas import tpu as pltpu
from jax.sharding import PartitionSpec as P

HEADS = 8
WIDTH = 128
TILE = 128
BAND = 2
NG = 4
ROWS = 512
TILES = ROWS // TILE
HALO = BAND * TILE
GSTRIDE = 768
LOG2E = 1.4426950408889634
SCALE = WIDTH**-0.5 * LOG2E
MASKED = -1e30
NX, NY, NZ, NC = 4, 8, 12, 2
ZL, ZH = 4, 3
YROWS = TILE // NY
ZHEADS = HEADS // ZL
MESH = pl.DeviceIdType.MESH


def place(x, y, z, c):
    return ((x * 4 + y % 4) * NC + c, (y // 4) * NZ + z)


def kernel(
    lists, order_row, k_in, v_in, q_in, out,
    raw, perm, qs, kbuf, vbuf, cand, core_in, half, y_in, chunk, z_in, zsum, zz_in, gbuf,
    peak, mass, acc, att, outv,
    in_sem, out_sem, halo_s, halo_r, core_s, core_r, y_s, y_r, z_s, z_r, zz_s, zz_r,
    za_s, za_r, ya_s, ya_r, xa_s, xa_r, ca_s, ca_r,
):
    blk, grp = lax.axis_index("blk"), lax.axis_index("grp")
    x, yl, c = blk // 8, blk // 2 % 4, blk % 2
    yh, z = grp // NZ, grp % NZ
    y = yh * 4 + yl
    zl, zh = z % ZL, z // ZL
    flat = blk * 24 + grp

    def along(step):
        other = (flat + step + 768) % 768
        return (other // 24, other % 24)

    def remote(src, dst, send, recv, device):
        return pltpu.make_async_remote_copy(
            src_ref=src, dst_ref=dst, send_sem=send, recv_sem=recv, device_id=device, device_id_type=MESH
        )

    loads = [
        pltpu.make_async_copy(src, raw.at[i], in_sem.at[i]) for i, src in enumerate((k_in, v_in, q_in))
    ]
    for load in loads:
        load.start()

    before, after, other_core = along(-1), along(1), place(x, y, z, 1 - c)
    y_to = [place(x, (y + d) % NY, z, c) for d in range(1, NY)]
    z_to = [place(x, y, zh * ZL + (zl + d) % ZL, c) for d in range(1, ZL)]
    zz_to = [place(x, y, (z + ZL * d) % NZ, c) for d in range(1, ZH)]
    x_to = [place((x + d) % NX, y, z, c) for d in range(1, NX)]
    partners = [before, after, other_core, *y_to, *z_to, *zz_to, *x_to]
    barrier = pltpu.get_barrier_semaphore()
    for partner in partners:
        pl.semaphore_signal(barrier, inc=1, device_id=partner, device_id_type=MESH)

    row = lax.rem(order_row[...], ROWS)
    wide = jnp.broadcast_to(row, (TILE, ROWS)).T
    lane = lax.broadcasted_iota(jnp.int32, (ROWS, TILE), 1)
    for b in range(TILES):
        perm[:, b * TILE : (b + 1) * TILE] = jnp.where(wide == lane + b * TILE, 1.0, 0.0).astype(jnp.bfloat16)

    def sort(which, dst, first):
        def pair(i, carry):
            cols = pl.ds(pl.multiple_of(i * 256, 256), 256)
            both = jnp.dot(perm[...], raw[which, :, cols], preferred_element_type=jnp.float32)
            both = both.astype(jnp.bfloat16)
            dst[2 * i, first : first + ROWS, :] = both[:, :WIDTH]
            dst[2 * i + 1, first : first + ROWS, :] = both[:, WIDTH:]
            return carry

        lax.fori_loop(0, HEADS // 2, pair, 0)

    def halo_copies(i, buf):
        return [
            remote(buf.at[:, pl.ds(HALO, HALO)], buf.at[:, pl.ds(HALO + ROWS, HALO)], halo_s.at[2 * i], halo_r.at[2 * i], before),
            remote(buf.at[:, pl.ds(ROWS, HALO)], buf.at[:, pl.ds(0, HALO)], halo_s.at[2 * i + 1], halo_r.at[2 * i + 1], after),
        ]

    loads[0].wait()
    sort(0, kbuf, HALO)
    pl.semaphore_wait(barrier, len(partners))
    halo_k = halo_copies(0, kbuf)
    for copy in halo_k:
        copy.start()
    loads[1].wait()
    sort(1, vbuf, HALO)
    halo_v = halo_copies(1, vbuf)
    for copy in halo_v:
        copy.start()

    spot = lax.rem(lists[0, 2 * BAND + 1], GSTRIDE)
    mine = lax.div(spot, TILES) == flat % (GSTRIDE // TILES)
    parts = [jnp.where(mine & (lax.rem(spot, TILES) == t), 1.0, 0.0).astype(jnp.float32) for t in range(TILES)]

    def candidate(h, carry):
        for i, buf in enumerate((kbuf, vbuf)):
            total = None
            for t in range(TILES):
                term = buf[h, HALO + t * TILE : HALO + (t + 1) * TILE, :].astype(jnp.float32) * parts[t]
                total = term if total is None else total + term
            cand[i, h] = total.astype(jnp.bfloat16)
        return carry

    lax.fori_loop(0, HEADS, candidate, 0)
    core_copy = remote(cand.at[1 - c], core_in, core_s, core_r, other_core)
    core_copy.start()

    loads[2].wait()
    sort(2, qs, 0)

    core_copy.wait_recv()
    half[...] = cand[c] + core_in[...]
    y_copies = []
    for d in range(1, NY):
        rows = pl.ds(pl.multiple_of((y + d) % NY * YROWS, YROWS), YROWS)
        copy = remote(half.at[:, rows], y_in.at[d - 1], y_s.at[d - 1], y_r.at[d - 1], y_to[d - 1])
        copy.start()
        y_copies.append(copy)

    ones = jnp.ones((1, WIDTH), jnp.bfloat16)

    def weigh(q, k, v, biases):
        scores = lax.dot_general(q, k, (((1,), (1,)), ((), ())), preferred_element_type=jnp.float32) * SCALE
        if biases is not None:
            scores = jnp.concatenate(
                [scores[:, i * TILE : (i + 1) * TILE] + bias for i, bias in enumerate(biases)], axis=1
            )
        return scores

    def widened(v):
        return jnp.concatenate([v, jnp.broadcast_to(ones, v.shape)], axis=1)

    def bias_of(t, b):
        return jnp.where(lists[t, b - t + BAND] >= 0, 0.0, MASKED).astype(jnp.float32)

    def local(h, carry):
        for t in range(TILES):
            low, high = max(0, t - BAND), min(TILES, t + BAND + 1)
            keys = slice(HALO + low * TILE, HALO + high * TILE)
            here = slice(t * TILE, (t + 1) * TILE)
            scores = weigh(qs[h, here], kbuf[h, keys], None, [bias_of(t, b) for b in range(low, high)])
            top = jnp.broadcast_to(jnp.max(scores, axis=1, keepdims=True), (TILE, WIDTH))
            weights = jnp.exp2(scores - jnp.tile(top, (1, high - low))).astype(jnp.bfloat16)
            got = jnp.dot(weights, widened(vbuf[h, keys]), preferred_element_type=jnp.float32)
            peak[h, here] = top
            acc[h, here] = got[:, :WIDTH]
            mass[h, here] = got[:, WIDTH:]
        return carry

    def update(h, t, k, v, biases):
        here = slice(t * TILE, (t + 1) * TILE)
        scores = weigh(qs[h, here], k, None, biases)
        old = peak[h, here]
        top = jnp.maximum(old, jnp.broadcast_to(jnp.max(scores, axis=1, keepdims=True), (TILE, WIDTH)))
        weights = jnp.exp2(scores - jnp.tile(top, (1, k.shape[0] // TILE))).astype(jnp.bfloat16)
        got = jnp.dot(weights, widened(v), preferred_element_type=jnp.float32)
        keep = jnp.exp2(old - top)
        return top, acc[h, here] * keep + got[:, :WIDTH], mass[h, here] * keep + got[:, WIDTH:]

    lax.fori_loop(0, 2, local, 0)

    for copy in y_copies:
        copy.wait_recv()
    total = half[:, pl.ds(pl.multiple_of(y * YROWS, YROWS), YROWS)]
    for d in range(1, NY):
        total = total + y_in[d - 1]
    chunk[...] = total
    z_copies = []
    for d in range(1, ZL):
        heads = pl.ds((zl + d) % ZL * ZHEADS, ZHEADS)
        copy = remote(chunk.at[heads], z_in.at[d - 1], z_s.at[d - 1], z_r.at[d - 1], z_to[d - 1])
        copy.start()
        z_copies.append(copy)

    lax.fori_loop(2, 4, local, 0)

    for copy in z_copies:
        copy.wait_recv()
    zsum[...] = chunk[pl.ds(zl * ZHEADS, ZHEADS)] + z_in[0] + z_in[1] + z_in[2]
    zz_copies = []
    for d in range(1, ZH):
        copy = remote(zsum, zz_in.at[d - 1], zz_s.at[d - 1], zz_r.at[d - 1], zz_to[d - 1])
        copy.start()
        zz_copies.append(copy)

    lax.fori_loop(4, 6, local, 0)

    for copy in zz_copies:
        copy.wait_recv()
    own = gbuf.at[c, x, y, pl.ds(zl * ZHEADS, ZHEADS)]
    gbuf[c, x, y, pl.ds(zl * ZHEADS, ZHEADS)] = zsum[...] + zz_in[0] + zz_in[1]
    za_copies = []
    for d in range(1, ZL):
        copy = remote(own, own, za_s.at[d - 1], za_r.at[d - 1], z_to[d - 1])
        copy.start()
        za_copies.append(copy)

    lax.fori_loop(6, 8, local, 0)

    for copy in za_copies:
        copy.wait_recv()
    ya_copies = []
    for d in range(1, NY):
        copy = remote(gbuf.at[c, x, y], gbuf.at[c, x, y], ya_s.at[d - 1], ya_r.at[d - 1], y_to[d - 1])
        copy.start()
        ya_copies.append(copy)
    for copy in ya_copies:
        copy.wait_recv()
    xa_copies = []
    for d in range(1, NX):
        copy = remote(gbuf.at[c, x], gbuf.at[c, x], xa_s.at[d - 1], xa_r.at[d - 1], x_to[d - 1])
        copy.start()
        xa_copies.append(copy)
    ca_copies = []

    def hand_over(i, d):
        tile = gbuf.at[c, (x - d + NX) % NX]
        copy = remote(tile, tile, ca_s.at[i], ca_r.at[i], other_core)
        copy.start()
        ca_copies.append(copy)

    hand_over(0, 0)
    for d in range(1, NX):
        xa_copies[d - 1].wait_recv()
        hand_over(d, d)
    for copy in ca_copies:
        copy.wait_recv()

    def globals_(h, carry):
        k = gbuf[0, :, :, h].reshape(NG * TILE, WIDTH)
        v = gbuf[1, :, :, h].reshape(NG * TILE, WIDTH)
        for t in range(TILES):
            here = slice(t * TILE, (t + 1) * TILE)
            top, sums, share = update(h, t, k, v, None)
            peak[h, here] = top
            acc[h, here] = sums
            mass[h, here] = share
        return carry

    lax.fori_loop(0, HEADS, globals_, 0)

    for copy in halo_k + halo_v:
        copy.wait_recv()

    def edges(h, carry):
        cols = pl.ds(pl.multiple_of(h * WIDTH, WIDTH), WIDTH)
        for t in range(TILES):
            low, high = (t - BAND, 0) if t < BAND else (TILES, t + BAND + 1)
            keys = slice(HALO + low * TILE, HALO + high * TILE)
            biases = [bias_of(t, b) for b in range(low, high)]
            top, sums, share = update(h, t, kbuf[h, keys], vbuf[h, keys], biases)
            att[t * TILE : (t + 1) * TILE, cols] = (sums / share).astype(jnp.bfloat16)
        return carry

    lax.fori_loop(0, HEADS, edges, 0)

    sub = lax.broadcasted_iota(jnp.int32, (ROWS, ROWS), 0)
    perm[...] = jnp.where(jnp.broadcast_to(row, (ROWS, ROWS)) == sub, 1.0, 0.0).astype(jnp.bfloat16)
    stores = []
    for i in range(HEADS // 2):
        cols = slice(i * 256, (i + 1) * 256)
        outv[:, cols] = jnp.dot(perm[...], att[:, cols], preferred_element_type=jnp.float32).astype(jnp.bfloat16)
        store = pltpu.make_async_copy(outv.at[:, cols], out.at[:, cols], out_sem.at[i])
        store.start()
        stores.append(store)
    for copy in halo_k + halo_v + [core_copy] + y_copies + z_copies + zz_copies + za_copies + ya_copies + xa_copies + ca_copies:
        copy.wait_send()
    for store in stores:
        store.wait()


def body(query_rows, key_rows, value_rows, tile_lists, hilbert_order):
    bf16, f32, dma = jnp.bfloat16, jnp.float32, pltpu.SemaphoreType.DMA
    vmem = pltpu.VMEM
    features = HEADS * WIDTH
    padded = ROWS + 2 * HALO
    scratch = [
        vmem((3, ROWS, features), bf16),
        vmem((ROWS, ROWS), bf16),
        vmem((HEADS, ROWS, WIDTH), bf16),
        vmem((HEADS, padded, WIDTH), bf16),
        vmem((HEADS, padded, WIDTH), bf16),
        vmem((2, HEADS, TILE, WIDTH), bf16),
        vmem((HEADS, TILE, WIDTH), bf16),
        vmem((HEADS, TILE, WIDTH), bf16),
        vmem((NY - 1, HEADS, YROWS, WIDTH), bf16),
        vmem((HEADS, YROWS, WIDTH), bf16),
        vmem((ZL - 1, ZHEADS, YROWS, WIDTH), bf16),
        vmem((ZHEADS, YROWS, WIDTH), bf16),
        vmem((ZH - 1, ZHEADS, YROWS, WIDTH), bf16),
        vmem((2, NX, NY, HEADS, YROWS, WIDTH), bf16),
        vmem((HEADS, ROWS, WIDTH), f32),
        vmem((HEADS, ROWS, WIDTH), f32),
        vmem((HEADS, ROWS, WIDTH), f32),
        vmem((ROWS, features), bf16),
        vmem((ROWS, features), bf16),
        dma((3,)),
        dma((HEADS // 2,)),
        dma((4,)),
        dma((4,)),
        dma,
        dma,
    ]
    for count in (NY - 1, ZL - 1, ZH - 1, ZL - 1, NY - 1, NX - 1, NX):
        scratch += [dma((count,)), dma((count,))]
    anywhere = pl.BlockSpec(memory_space=pl.ANY)
    return pl.pallas_call(
        kernel,
        out_shape=jax.ShapeDtypeStruct(query_rows.shape, bf16),
        in_specs=[
            pl.BlockSpec(memory_space=pltpu.SMEM),
            pl.BlockSpec(memory_space=pltpu.VMEM),
            anywhere,
            anywhere,
            anywhere,
        ],
        out_specs=anywhere,
        scratch_shapes=scratch,
        compiler_params=pltpu.CompilerParams(
            collective_id=0, has_side_effects=True, vmem_limit_bytes=60 << 20
        ),
        name="attend",
    )(tile_lists, hilbert_order.reshape(1, ROWS), key_rows, value_rows, query_rows)


def solution(mesh):
    in_specs = (
        P(("blk", "grp"), None),
        P(("blk", "grp"), None),
        P(("blk", "grp"), None),
        P(("blk", "grp"), None),
        P(("blk", "grp")),
    )
    out_specs = P(("blk", "grp"), None)
    return jax.shard_map(body, mesh=mesh, in_specs=in_specs, out_specs=out_specs, check_vma=False)
```

time: 733 us -> 137 us (0.19)
  waiting for transfers between devices: 519 us -> 0 us
  Pallas kernels: 0 us -> 135 us
  local copies, waits for them, and re-layouts: 102 us -> 2.26 us
  matrix products: 48.7 us -> 0 us
  between operations: 23.7 us -> 0.01 us
  starting transfers between devices: 23.1 us -> 0 us
  other arithmetic: 9.93 us -> 0 us
    psum x1 -> x0, waiting for transfers between devices: 519 us -> none  [spread(): return lax.psum(jnp.where(mine, array, jnp.zeros_like(array)), axis)]
    pallas_call x0 -> x1, Pallas kernels: none -> 135 us  [body(): pl.pallas_call(kernel, out_shape=jax.ShapeDtypeStruct(query_rows.shape, b...]
    dot_general x8 -> x0, matrix products: 38.4 us -> none  [the longest x4 26.4 us: one_tile(): jnp.einsum('hqk,khd->qhd', weights, value_heads, preferred_element_type=j...]
    dynamic_slice x16 -> x0, local copies, waits for them, and re-layouts: 38.1 us -> none  [the longest x8 31.9 us: one_tile(): lax.dynamic_slice_in_dim(padded, tile_number * TILE_POINTS, (2 * BAND + 1...]
    while x28 -> x0, local copies, waits for them, and re-layouts: 32.4 us -> none
    ppermute x2 -> x0, starting transfers between devices: 23 us -> none  [the longest x1 18.2 us: extended(): lax.ppermute(lax.slice_in_dim(block, 0, width, axis=dim), axis, backward)]
    sub x4 -> x0, matrix products: 10.3 us -> none  [one_tile(): exponent = jnp.exp(scores - row_peak)]
    slice x5 -> x0, local copies, waits for them, and re-layouts: 8.49 us -> none  [the longest x4 6.99 us: one_tile(): key_heads = kv_here[0].reshape(-1, LOCAL_HEADS, HEAD_WIDTH)]
  transfers between devices with their start and end apart: 3 -> 0, of which waited for: 1 -> 0; matrix products, arithmetic and copies ran while one was open for 2% -> 0% of each run, Pallas kernels for 0% -> 0%
where the time goes in v1:
time: 137 us
  Pallas kernels  135 us (99%)
  local copies, waits for them, and re-layouts  2.26 us (2%)
    pallas_call x1, Pallas kernels, body(): pl.pallas_call(kernel, out_shape=jax.ShapeDtypeStruct(query_rows.shape, b...  135 us

profile of v1, /device:TPU:1, one launch (start us, length us, event | category | flops | bytes accessed | tf_op | source)
XLA Modules:
  0.0 136.8 jit_solution(8280047320480982028)
XLA Ops:
  0.0 134.6 %attend.1 = bf16[512,1024]{1,0:T(8,128)(2,1)} custom-call(s32[4,9]{1,0:T(4,128)} %lists.1, s32[1,512]{1,0:T(1,128)} %bitcast.1, bf16[512,1024]{1,0:T(8,128)(2,1)} %k_in.1, bf16[512,1024]{1,0:T(8,128)(2,1)} %v_in.1, bf16[512,1024]{1,0:T(8,128)(2,1)} %q_in.1), custom_call_target="tpu_custom_call" | custom-call | tf_op jit(solution)/shard_map/attend/pallas_call | solution.py:323
  134.6 2.3 %copy.7 = bf16[512,1024]{1,0:T(8,128)(2,1)} copy(bf16[512,1024]{1,0:T(8,128)(2,1)} %attend.1) | data formatting | bytes 2097152

commit v2 on v1

v2 whole, which is shorter than its diff:
```python
import functools

import jax
import jax.numpy as jnp
from jax import lax
from jax.experimental import pallas as pl
from jax.experimental.pallas import tpu as pltpu
from jax.sharding import PartitionSpec as P

HEADS = 8
WIDTH = 128
TILE = 128
BAND = 2
NG = 4
ROWS = 512
TILES = ROWS // TILE
HALO = BAND * TILE
GSTRIDE = 768
LOG2E = 1.4426950408889634
SCALE = WIDTH**-0.5 * LOG2E
MASKED = -1e30
NX, NY, NZ, NC = 4, 8, 12, 2
YROWS = TILE // NY
GROUP, OWNERS = 6, 4
OWN = HEADS // OWNERS
OWNER_PLANES = tuple(range(GROUP - OWNERS, GROUP + OWNERS))
DIRECT = 4
RELAYS = (9, 10, 2, 1)
NEAR_FIRST = True
MESH = pl.DeviceIdType.MESH


def place(x, y, z, c):
    return ((x * 4 + y % 4) * NC + c, (y // 4) * NZ + z)


def kernel(
    lists, order_row, k_in, v_in, q_in, out,
    raw, perm, picked, qs, kbuf, vbuf, relayed, cand, core_in, half, z_in, zsum, y_in, ysum, zz_in, gbuf,
    peak, mass, acc, att, outv,
    in_sem, out_sem, near_s, halo_r, leg_s, leg_r, relay_s, core_s, core_r, z_s, z_r, y_s, y_r, zz_s, zz_r,
    ya_s, ya_r, za_s, za_r, xa_s, xa_r, ca_s, ca_r,
):
    blk, grp = lax.axis_index("blk"), lax.axis_index("grp")
    x, yl, c = blk // 8, blk // 2 % 4, blk % 2
    yh, z = grp // NZ, grp % NZ
    y = yh * 4 + yl
    flat = blk * 24 + grp
    base = jnp.where(z < GROUP, GROUP - OWNERS, GROUP)
    first, member, own = z // GROUP * GROUP, z % GROUP, z - base
    owner = (own >= 0) & (own < OWNERS)

    def along(step):
        other = (flat + step + 768) % 768
        return (other // 24, other % 24)

    def remote(src, dst, send, recv, device):
        return pltpu.make_async_remote_copy(
            src_ref=src, dst_ref=dst, send_sem=send, recv_sem=recv, device_id=device, device_id_type=MESH
        )

    loads = [
        pltpu.make_async_copy(src, raw.at[i], in_sem.at[i]) for i, src in enumerate((k_in, v_in, q_in))
    ]
    for load in loads:
        load.start()

    other_core = place(x, y, z, 1 - c)
    y_to = [place(x, y + d - jnp.where(y + d >= NY, NY, 0), z, c) for d in range(1, NY)]
    x_to = [place((x + d) % NX, y, z, c) for d in range(1, NX)]
    partner = place(x, y, jnp.where(z < GROUP, z + 4, z - 4), c)
    barrier = pltpu.get_barrier_semaphore()

    def in_group(m):
        return place(x, y, first + m, c)

    def owner_of(k):
        return place(x, y, base + k, c)

    def greet(devices):
        for device in devices:
            pl.semaphore_signal(barrier, inc=1, device_id=device, device_id_type=MESH)

    own_next = [(own + d) % OWNERS for d in range(1, OWNERS)]
    idle = jnp.where(z < GROUP, 0, 10)
    owner_greets = [*y_to, partner, *[owner_of(k) for k in own_next], place(x, y, idle, c), place(x, y, idle + 1, c)]
    other_greets = [owner_of(k) for k in range(OWNERS)]
    after_greets = [along(step) for r in RELAYS for step in (1 + r, r - 11)]
    before_greets = [along(step) for r in RELAYS for step in (r - 12, r)]
    common = [along(-1), along(1), other_core, *x_to]
    greet(common)
    pl.when(owner)(lambda: greet(owner_greets))
    pl.when(jnp.logical_not(owner))(lambda: greet(other_greets))
    pl.when(z == NZ - 1)(lambda: greet(after_greets))
    pl.when(z == 0)(lambda: greet(before_greets))
    for r in RELAYS:
        pl.when(z == r)(functools.partial(greet, [along(step) for step in (-r, 11 - r, -r - 1, 12 - r)]))

    def greeted():
        for plane in range(NZ):
            count = len(common)
            count += len(owner_greets) if plane in OWNER_PLANES else len(other_greets)
            count += 2 * len(RELAYS) if plane in (0, NZ - 1) else 0
            count += 4 if plane in RELAYS else 0
            pl.when(z == plane)(functools.partial(pl.semaphore_wait, barrier, count))

    row = lax.rem(order_row[...], ROWS)
    wide = jnp.broadcast_to(row, (TILE, ROWS)).T
    lane = lax.broadcasted_iota(jnp.int32, (ROWS, TILE), 1)
    for b in range(TILES):
        perm[:, b * TILE : (b + 1) * TILE] = jnp.where(wide == lane + b * TILE, 1.0, 0.0).astype(jnp.bfloat16)

    def sort(which, dst, start):
        def pair(i, carry):
            cols = pl.ds(pl.multiple_of(i * 256, 256), 256)
            both = jnp.dot(perm[...], raw[which, :, cols], preferred_element_type=jnp.float32)
            both = both.astype(jnp.bfloat16)
            dst[2 * i, start : start + ROWS, :] = both[:, :WIDTH]
            dst[2 * i + 1, start : start + ROWS, :] = both[:, WIDTH:]
            return carry

        lax.fori_loop(0, HEADS // 2, pair, 0)

    bufs = (kbuf, vbuf)
    send_rows = (pl.ds(ROWS, HALO), pl.ds(HALO, HALO))
    land_rows = (pl.ds(0, HALO), pl.ds(HALO + ROWS, HALO))

    def straight(i, way, heads):
        here = pl.ds(0, heads)
        return remote(
            bufs[i].at[here, send_rows[way]], bufs[i].at[here, land_rows[way]],
            near_s.at[i, way], halo_r.at[i, way, 0], along(1 - 2 * way),
        )

    def to_relay(i, way, p):
        return remote(
            bufs[i].at[DIRECT + p, send_rows[way]], relayed.at[i, way],
            leg_s.at[i, p], leg_r.at[i, way], along(RELAYS[p] + (1, -12)[way]),
        )

    def from_relay(i, way, p):
        return remote(
            relayed.at[i, way], bufs[i].at[DIRECT + p, land_rows[way]],
            relay_s.at[i, way], halo_r.at[i, way, p + 1], along((0, 11)[way] - RELAYS[p]),
        )

    edges = ((NZ - 1, 0), (0, 1))
    seam_in = (0, NZ - 1)

    def send_far(i):
        for plane, way in edges:
            @pl.when(z == plane)
            def _():
                for p in range(len(RELAYS)):
                    to_relay(i, way, p).start()
                straight(i, way, DIRECT).start()

    def send_near(i):
        for plane, way in edges:
            pl.when(z != plane)(lambda: straight(i, way, HEADS).start())

    def forward(i):
        for p, r in enumerate(RELAYS):
            @pl.when(z == r)
            def _():
                for way in (0, 1) if r >= GROUP else (1, 0):
                    to_relay(i, way, p).wait_recv()
                    from_relay(i, way, p).start()

    def halo_sent():
        for i in range(2):
            for plane, way in edges:
                @pl.when(z == plane)
                def _():
                    for p in range(len(RELAYS)):
                        to_relay(i, way, p).wait_send()
                    straight(i, way, DIRECT).wait_send()

                pl.when(z != plane)(lambda: straight(i, way, HEADS).wait_send())
            for p, r in enumerate(RELAYS):
                @pl.when(z == r)
                def _():
                    for way in range(2):
                        from_relay(i, way, p).wait_send()

    def halo_landed(way, far):
        @pl.when((z == seam_in[way]) == far)
        def _():
            for i in range(2):
                if far:
                    straight(i, way, DIRECT).wait_recv()
                    for p in range(len(RELAYS)):
                        from_relay(i, way, p).wait_recv()
                else:
                    straight(i, way, HEADS).wait_recv()

    spot = lax.rem(lists[0, 2 * BAND + 1], GSTRIDE)
    mine = lax.div(spot, TILES) == flat % (GSTRIDE // TILES)
    parts = [jnp.where(mine & (lax.rem(spot, TILES) == t), 1.0, 0.0).astype(jnp.bfloat16) for t in range(TILES)]
    pick = None
    for t in range(TILES):
        term = perm[t * TILE : (t + 1) * TILE, :] * parts[t]
        pick = term if pick is None else pick + term
    picked[...] = pick

    def candidate(i):
        def pair(j, carry):
            cols = pl.ds(pl.multiple_of(j * 256, 256), 256)
            both = jnp.dot(picked[...], raw[i, :, cols], preferred_element_type=jnp.float32).astype(jnp.bfloat16)
            cand[i, 2 * j] = both[:, :WIDTH]
            cand[i, 2 * j + 1] = both[:, WIDTH:]
            return carry

        lax.fori_loop(0, HEADS // 2, pair, 0)

    loads[0].wait()
    candidate(0)
    loads[1].wait()
    candidate(1)
    greeted()
    core_copy = remote(cand.at[1 - c], core_in, core_s, core_r, other_core)
    core_copy.start()
    sort(0, kbuf, HALO)
    send_far(0)
    core_copy.wait_recv()
    half[...] = cand[c] + core_in[...]

    def z_copy(i, k):
        return remote(half.at[pl.ds(k * OWN, OWN)], z_in.at[member], z_s.at[i], z_r.at[member], owner_of(k))

    @pl.when(owner)
    def _():
        for i, k in enumerate(own_next):
            z_copy(i, k).start()
        z_in[member] = half[pl.ds(own * OWN, OWN)]

    @pl.when(jnp.logical_not(owner))
    def _():
        for k in range(OWNERS):
            z_copy(k, k).start()

    sort(1, vbuf, HALO)
    send_far(1)
    loads[2].wait()
    sort(2, qs, 0)

    ones = jnp.ones((1, WIDTH), jnp.bfloat16)

    def scored(q, k, biases):
        scores = lax.dot_general(q, k, (((1,), (1,)), ((), ())), preferred_element_type=jnp.float32) * SCALE
        if biases is not None:
            scores = jnp.concatenate(
                [scores[:, i * TILE : (i + 1) * TILE] + bias for i, bias in enumerate(biases)], axis=1
            )
        return scores

    def widened(v):
        return jnp.concatenate([v, jnp.broadcast_to(ones, v.shape)], axis=1)

    def bias_of(t, b):
        return jnp.where(lists[t, b - t + BAND] >= 0, 0.0, MASKED).astype(jnp.float32)

    def local(h, carry):
        for t in range(TILES):
            low, high = max(0, t - BAND), min(TILES, t + BAND + 1)
            keys = slice(HALO + low * TILE, HALO + high * TILE)
            here = slice(t * TILE, (t + 1) * TILE)
            scores = scored(qs[h, here], kbuf[h, keys], [bias_of(t, b) for b in range(low, high)])
            top = jnp.broadcast_to(jnp.max(scores, axis=1, keepdims=True), (TILE, WIDTH))
            weights = jnp.exp2(scores - jnp.tile(top, (1, high - low))).astype(jnp.bfloat16)
            got = jnp.dot(weights, widened(vbuf[h, keys]), preferred_element_type=jnp.float32)
            peak[h, here] = top
            acc[h, here] = got[:, :WIDTH]
            mass[h, here] = got[:, WIDTH:]
        return carry

    def update(h, t, k, v, biases):
        here = slice(t * TILE, (t + 1) * TILE)
        scores = scored(qs[h, here], k, biases)
        old = peak[h, here]
        top = jnp.maximum(old, jnp.broadcast_to(jnp.max(scores, axis=1, keepdims=True), (TILE, WIDTH)))
        weights = jnp.exp2(scores - jnp.tile(top, (1, k.shape[0] // TILE))).astype(jnp.bfloat16)
        got = jnp.dot(weights, widened(v), preferred_element_type=jnp.float32)
        keep = jnp.exp2(old - top)
        return top, acc[h, here] * keep + got[:, :WIDTH], mass[h, here] * keep + got[:, WIDTH:]

    lax.fori_loop(0, 2, local, 0)

    def y_copy(d):
        rows = pl.ds(pl.multiple_of((y + d) % NY * YROWS, YROWS), YROWS)
        return remote(zsum.at[:, rows], y_in.at[d - 1], y_s.at[d - 1], y_r.at[d - 1], y_to[d - 1])

    @pl.when(owner)
    def _():
        for m in range(GROUP):
            @pl.when(member != m)
            def _():
                remote(half.at[pl.ds(0, OWN)], z_in.at[m], z_s.at[0], z_r.at[m], in_group(m)).wait_recv()

        zsum[...] = ((z_in[0] + z_in[1]) + (z_in[2] + z_in[3])) + (z_in[4] + z_in[5])
        for d in range(1, NY):
            y_copy(d).start()

    send_near(0)
    send_near(1)
    forward(0)
    lax.fori_loop(2, 4, local, 0)

    zz_copy = remote(ysum, zz_in, zz_s, zz_r, partner)

    @pl.when(owner)
    def _():
        for d in range(1, NY):
            y_copy(d).wait_recv()
        total = zsum[:, pl.ds(pl.multiple_of(y * YROWS, YROWS), YROWS)]
        for d in range(1, NY):
            total = total + y_in[d - 1]
        ysum[...] = total
        zz_copy.start()

    forward(1)
    lax.fori_loop(4, 6, local, 0)

    k_here = lax.rem(own + OWNERS, OWNERS)
    rows_here = gbuf.at[c, x, k_here, y]

    def ya_copy(d):
        return remote(rows_here, rows_here, ya_s.at[d - 1], ya_r.at[d - 1], y_to[d - 1])

    @pl.when(owner)
    def _():
        zz_copy.wait_recv()
        gbuf[c, x, k_here, y] = ysum[...] + zz_in[...]
        for d in range(1, NY):
            ya_copy(d).start()

    lax.fori_loop(6, 8, local, 0)

    def za_copy(m):
        piece = gbuf.at[c, x, k_here]
        return remote(piece, piece, za_s.at[m], za_r.at[k_here], in_group(m))

    @pl.when(owner)
    def _():
        for d in range(1, NY):
            ya_copy(d).wait_recv()
        for m in range(GROUP):
            pl.when(member != m)(lambda: za_copy(m).start())

    def xa_copy(k, d):
        piece = gbuf.at[c, x, k]
        return remote(piece, piece, xa_s.at[k, d - 1], xa_r.at[k, d - 1], x_to[d - 1])

    def ca_copy(k, d):
        piece = gbuf.at[c, (x - d + NX) % NX, k]
        return remote(piece, piece, ca_s.at[k, d], ca_r.at[k, d], other_core)

    for k in range(OWNERS):
        @pl.when(own != k)
        def _():
            piece = gbuf.at[c, x, k]
            remote(piece, piece, za_s.at[0], za_r.at[k], in_group(0)).wait_recv()

        for d in range(1, NX):
            xa_copy(k, d).start()
        ca_copy(k, 0).start()

    def side(way, last):
        def head(h, carry):
            cols = pl.ds(pl.multiple_of(h * WIDTH, WIDTH), WIDTH)
            for t in (0, 1) if way == 0 else (2, 3):
                low, high = (t - BAND, 0) if way == 0 else (TILES, t + BAND + 1)
                keys = slice(HALO + low * TILE, HALO + high * TILE)
                here = slice(t * TILE, (t + 1) * TILE)
                biases = [bias_of(t, b) for b in range(low, high)]
                top, sums, share = update(h, t, kbuf[h, keys], vbuf[h, keys], biases)
                if last:
                    att[here, cols] = (sums / share).astype(jnp.bfloat16)
                else:
                    peak[h, here] = top
                    acc[h, here] = sums
                    mass[h, here] = share
            return carry

        lax.fori_loop(0, HEADS, head, 0)

    def near_side():
        for way in range(2):
            @pl.when((z == 0) == (way == 1))
            def _():
                halo_landed(way, False)
                side(way, not NEAR_FIRST)

    def globals_(h, carry):
        k = gbuf[0, :, h // OWN, :, h % OWN].reshape(NG * TILE, WIDTH)
        v = gbuf[1, :, h // OWN, :, h % OWN].reshape(NG * TILE, WIDTH)
        cols = pl.ds(pl.multiple_of(h * WIDTH, WIDTH), WIDTH)
        for t in range(TILES):
            here = slice(t * TILE, (t + 1) * TILE)
            top, sums, share = update(h, t, k, v, None)
            peak[h, here] = top
            acc[h, here] = sums
            mass[h, here] = share
            if NEAR_FIRST:
                att[here, cols] = (sums / share).astype(jnp.bfloat16)
        return carry

    if NEAR_FIRST:
        near_side()
    for k in range(OWNERS + 1):
        if k < OWNERS:
            for d in range(1, NX):
                xa_copy(k, d).wait_recv()
                ca_copy(k, d).start()
        if k > 0:
            for d in range(NX):
                ca_copy(k - 1, d).wait_recv()
            lax.fori_loop(OWN * (k - 1), OWN * k, globals_, 0)
    if not NEAR_FIRST:
        near_side()

    for way in range(2):
        @pl.when((z == 0) == (way == 0))
        def _():
            halo_landed(way, True)
            halo_landed(way, False)
            side(way, True)

    sub = lax.broadcasted_iota(jnp.int32, (ROWS, ROWS), 0)
    perm[...] = jnp.where(jnp.broadcast_to(row, (ROWS, ROWS)) == sub, 1.0, 0.0).astype(jnp.bfloat16)
    stores = []
    for i in range(HEADS // 2):
        cols = slice(i * 256, (i + 1) * 256)
        outv[:, cols] = jnp.dot(perm[...], att[:, cols], preferred_element_type=jnp.float32).astype(jnp.bfloat16)
        store = pltpu.make_async_copy(outv.at[:, cols], out.at[:, cols], out_sem.at[i])
        store.start()
        stores.append(store)
    halo_sent()

    @pl.when(owner)
    def _():
        for i, k in enumerate(own_next):
            z_copy(i, k).wait_send()
        for d in range(1, NY):
            y_copy(d).wait_send()
            ya_copy(d).wait_send()
        zz_copy.wait_send()
        for m in range(GROUP):
            pl.when(member != m)(lambda: za_copy(m).wait_send())

    @pl.when(jnp.logical_not(owner))
    def _():
        for k in range(OWNERS):
            z_copy(k, k).wait_send()

    core_copy.wait_send()
    for k in range(OWNERS):
        for d in range(1, NX):
            xa_copy(k, d).wait_send()
        for d in range(NX):
            ca_copy(k, d).wait_send()
    for store in stores:
        store.wait()


def body(query_rows, key_rows, value_rows, tile_lists, hilbert_order):
    bf16, f32, dma = jnp.bfloat16, jnp.float32, pltpu.SemaphoreType.DMA
    vmem = pltpu.VMEM
    features = HEADS * WIDTH
    padded = ROWS + 2 * HALO
    scratch = [
        vmem((3, ROWS, features), bf16),
        vmem((ROWS, ROWS), bf16),
        vmem((TILE, ROWS), bf16),
        vmem((HEADS, ROWS, WIDTH), bf16),
        vmem((HEADS, padded, WIDTH), bf16),
        vmem((HEADS, padded, WIDTH), bf16),
        vmem((2, 2, HALO, WIDTH), bf16),
        vmem((2, HEADS, TILE, WIDTH), bf16),
        vmem((HEADS, TILE, WIDTH), bf16),
        vmem((HEADS, TILE, WIDTH), bf16),
        vmem((GROUP, OWN, TILE, WIDTH), bf16),
        vmem((OWN, TILE, WIDTH), bf16),
        vmem((NY - 1, OWN, YROWS, WIDTH), bf16),
        vmem((OWN, YROWS, WIDTH), bf16),
        vmem((OWN, YROWS, WIDTH), bf16),
        vmem((2, NX, OWNERS, NY, OWN, YROWS, WIDTH), bf16),
        vmem((HEADS, ROWS, WIDTH), f32),
        vmem((HEADS, ROWS, WIDTH), f32),
        vmem((HEADS, ROWS, WIDTH), f32),
        vmem((ROWS, features), bf16),
        vmem((ROWS, features), bf16),
        dma((3,)),
        dma((HEADS // 2,)),
        dma((2, 2)),
        dma((2, 2, 1 + len(RELAYS))),
        dma((2, len(RELAYS))),
        dma((2, 2)),
        dma((2, 2)),
        dma,
        dma,
        dma((OWNERS,)),
        dma((GROUP,)),
        dma((NY - 1,)),
        dma((NY - 1,)),
        dma,
        dma,
        dma((NY - 1,)),
        dma((NY - 1,)),
        dma((GROUP,)),
        dma((OWNERS,)),
        dma((OWNERS, NX - 1)),
        dma((OWNERS, NX - 1)),
        dma((OWNERS, NX)),
        dma((OWNERS, NX)),
    ]
    anywhere = pl.BlockSpec(memory_space=pl.ANY)
    return pl.pallas_call(
        kernel,
        out_shape=jax.ShapeDtypeStruct(query_rows.shape, bf16),
        in_specs=[
            pl.BlockSpec(memory_space=pltpu.SMEM),
            pl.BlockSpec(memory_space=pltpu.VMEM),
            anywhere,
            anywhere,
            anywhere,
        ],
        out_specs=anywhere,
        scratch_shapes=scratch,
        compiler_params=pltpu.CompilerParams(
            collective_id=0, has_side_effects=True, vmem_limit_bytes=60 << 20
        ),
        name="attend",
    )(tile_lists, hilbert_order.reshape(1, ROWS), key_rows, value_rows, query_rows)


def solution(mesh):
    in_specs = (
        P(("blk", "grp"), None),
        P(("blk", "grp"), None),
        P(("blk", "grp"), None),
        P(("blk", "grp"), None),
        P(("blk", "grp")),
    )
    out_specs = P(("blk", "grp"), None)
    return jax.shard_map(body, mesh=mesh, in_specs=in_specs, out_specs=out_specs, check_vma=False)
```

time: 137 us -> 98.8 us (0.72)
  Pallas kernels: 135 us -> 96.4 us
    pallas_call x1, Pallas kernels: 135 us -> 96.4 us  [body(): pl.pallas_call(kernel, out_shape=jax.ShapeDtypeStruct(query_rows.shape, b...]
where the time goes in v2:
time: 98.8 us; the launch traced here: 98.7 us
  Pallas kernels  96.4 us (98%)
  local copies, waits for them, and re-layouts  2.26 us (2%)
    pallas_call x1, Pallas kernels, body(): pl.pallas_call(kernel, out_shape=jax.ShapeDtypeStruct(query_rows.shape, b...  96.4 us
    unnamed x1, local copies, waits for them, and re-layouts  2.26 us

profile of v2, /device:TPU:1, one launch (start us, length us, event | category | flops | bytes accessed | tf_op | source)
XLA Modules:
  0.0 98.7 jit_solution(7189398577054862815)
XLA Ops:
  0.0 96.4 %attend.1 = bf16[512,1024]{1,0:T(8,128)(2,1)} custom-call(s32[4,9]{1,0:T(4,128)} %lists.1, s32[1,512]{1,0:T(1,128)} %bitcast.1, bf16[512,1024]{1,0:T(8,128)(2,1)} %k_in.1, bf16[512,1024]{1,0:T(8,128)(2,1)} %v_in.1, bf16[512,1024]{1,0:T(8,128)(2,1)} %q_in.1), custom_call_target="tpu_custom_call" | custom-call | tf_op jit(solution)/shard_map/attend/pallas_call | solution.py:518
  96.4 2.3 %copy.7 = bf16[512,1024]{1,0:T(8,128)(2,1)} copy(bf16[512,1024]{1,0:T(8,128)(2,1)} %attend.1) | data formatting | bytes 2097152

commit v3 on v2

--- a/solution.py
+++ b/solution.py
@@ -26,7 +26,7 @@
 OWNER_PLANES = tuple(range(GROUP - OWNERS, GROUP + OWNERS))
 DIRECT = 4
 RELAYS = (9, 10, 2, 1)
-NEAR_FIRST = True
+NEAR_FIRST = False
 MESH = pl.DeviceIdType.MESH
 
 
@@ -221,7 +221,6 @@
     core_copy = remote(cand.at[1 - c], core_in, core_s, core_r, other_core)
     core_copy.start()
     sort(0, kbuf, HALO)
-    send_far(0)
     core_copy.wait_recv()
     half[...] = cand[c] + core_in[...]
 
@@ -239,6 +238,7 @@
         for k in range(OWNERS):
             z_copy(k, k).start()
 
+    send_far(0)
     sort(1, vbuf, HALO)
     send_far(1)
     loads[2].wait()
@@ -302,7 +302,6 @@
             y_copy(d).start()
 
     send_near(0)
-    send_near(1)
     forward(0)
     lax.fori_loop(2, 4, local, 0)
 
@@ -346,6 +345,8 @@
             ya_copy(d).wait_recv()
         for m in range(GROUP):
             pl.when(member != m)(lambda: za_copy(m).start())
+
+    send_near(1)
 
     def xa_copy(k, d):
         piece = gbuf.at[c, x, k]

time: 98.8 us -> 94.1 us (0.952)
  Pallas kernels: 96.4 us -> 91.6 us
    pallas_call x1, Pallas kernels: 96.4 us -> 91.6 us  [body(): pl.pallas_call(kernel, out_shape=jax.ShapeDtypeStruct(query_rows.shape, b...]
where the time goes in v3:
time: 94.1 us; the launch traced here: 93.9 us
  Pallas kernels  91.6 us (97%)
  local copies, waits for them, and re-layouts  2.26 us (2%)
    pallas_call x1, Pallas kernels, body(): pl.pallas_call(kernel, out_shape=jax.ShapeDtypeStruct(query_rows.shape, b...  91.6 us
    unnamed x1, local copies, waits for them, and re-layouts  2.26 us

profile of v3, /device:TPU:1, one launch (start us, length us, event | category | flops | bytes accessed | tf_op | source)
XLA Modules:
  0.0 93.9 jit_solution(16819974536753207678)
XLA Ops:
  0.0 91.6 %attend.1 = bf16[512,1024]{1,0:T(8,128)(2,1)} custom-call(s32[4,9]{1,0:T(4,128)} %lists.1, s32[1,512]{1,0:T(1,128)} %bitcast.1, bf16[512,1024]{1,0:T(8,128)(2,1)} %k_in.1, bf16[512,1024]{1,0:T(8,128)(2,1)} %v_in.1, bf16[512,1024]{1,0:T(8,128)(2,1)} %q_in.1), custom_call_target="tpu_custom_call" | custom-call | tf_op jit(solution)/shard_map/attend/pallas_call | solution.py:519
  91.6 2.3 %copy.7 = bf16[512,1024]{1,0:T(8,128)(2,1)} copy(bf16[512,1024]{1,0:T(8,128)(2,1)} %attend.1) | data formatting | bytes 2097152
